TPU v7x, 128 devices: a whole 4x4x4 slice. The times are simulated.
128 devices in a mesh: grp: 8 (over x, core), dev: 16 (over z, y).
Axes of the slice: x: 4, y: 4, z: 4, core: 2. Of those that a mesh axis runs over, the one named last changes fastest.
Arguments:
- residual: bfloat16 [16384, 2048], P(('grp', 'dev')), may hold values from -3 to 3
- queries: bfloat16 [16384, 1024], P(('grp', 'dev')), may hold values from -9 to 9
- keys: bfloat16 [16384, 256], P(('grp', 'dev')), may hold values from -6 to 6
- values: bfloat16 [16384, 256], P(('grp', 'dev')), may hold values from -18 to 18
- prefix_keys: bfloat16 [32, 1024, 256], P('grp', 'dev'), may hold values from -6 to 6
- cached_prefix_values: bfloat16 [32, 1024, 256], P('grp', 'dev'), may hold values from -18 to 18
- out_weight: bfloat16 [1024, 2048], replicated, may hold values from -0.1875 to 0.1875
- norm_gain: float32 [2048], replicated, may hold values from 0.25 to 1.75
- w_gate: bfloat16 [2048, 8192], P('grp', 'dev'), may hold values from -0.125 to 0.125
- w_up: bfloat16 [2048, 8192], P('grp', 'dev'), may hold values from -0.125 to 0.125
- w_down: bfloat16 [8192, 2048], P('dev', 'grp'), may hold values from -0.0625 to 0.0625
- suffix_lengths: int32 [8, 32], P('grp'), may hold values from 1 to 128, 2048 in all within a row
- request_group: int32 [8, 32], P('grp'), may hold values from 0 to 3, as said below
- placement_order: int32 [8, 32], P('grp'), may hold values from 0 to 31, each once within a row
Outputs:
- layer_out: bfloat16 [16384, 2048], P(('grp', 'dev'))
Inputs may be any that keep to these rules, and one draw needn't show every extreme that they name: `suffix_lengths`: the 32 lengths of one row sum to 2048. `request_group`: each row names each of its 4 groups exactly 8 times. `placement_order`: each row is an ordering of its 32 requests.
All inputs are finite; a program needn't handle non-finite values.
Results may differ from a plain program's by a relative error of at most 0.012.
Values may be sent and summed in bfloat16 or wider, within the bound.
A program may use at most 128 MiB of HBM per device.

v0:
```python
import math
import jax
import jax.numpy as jnp
from jax import lax
from jax.sharding import PartitionSpec as P

HEAD_SIZE = 64
NEG_FILL = -1e30
EPSILON = 1e-05


def row_layout(lengths, group_map, packed_order):
    request_count = lengths.shape[0]
    picked = (packed_order[:, None] == jnp.arange(request_count, dtype=jnp.int32)[None, :]).astype(
        jnp.int32
    )
    packed_len = jnp.sum(picked * lengths[None, :], axis=1)
    packed_group = jnp.sum(picked * group_map[None, :], axis=1)
    ends_at = jnp.cumsum(packed_len)
    return (ends_at - packed_len, ends_at, packed_group)


def token_info(token_rows, starts_at, ends_at, packed_group):
    inside = (
        (token_rows[:, None] >= starts_at[None, :]) & (token_rows[:, None] < ends_at[None, :])
    ).astype(jnp.int32)
    return (
        jnp.sum(inside * packed_group[None, :], axis=1),
        jnp.sum(inside * starts_at[None, :], axis=1),
    )


def block_partial(rows_of_queries, allowed, rows_of_keys, rows_of_values):
    query_row_count = rows_of_queries.shape[0]
    key_row_count = rows_of_keys.shape[0]
    heads_kv = rows_of_keys.shape[1] // HEAD_SIZE
    heads_of_queries = rows_of_queries.reshape(query_row_count, heads_kv, -1, HEAD_SIZE)
    heads_of_keys = rows_of_keys.reshape(key_row_count, heads_kv, HEAD_SIZE)
    heads_of_values = rows_of_values.reshape(key_row_count, heads_kv, HEAD_SIZE)
    scores = jnp.einsum(
        "nkrd,mkd->nkrm", heads_of_queries, heads_of_keys, preferred_element_type=jnp.float32
    ) * HEAD_SIZE ** (-0.5)
    scores = jnp.where(allowed[:, None, None, :], scores, NEG_FILL)
    maxima = jnp.max(scores, axis=-1)
    weights = jnp.exp(scores - maxima[..., None])
    totals = jnp.sum(weights, axis=-1)
    numerator = jnp.einsum(
        "nkrm,mkd->nkrd",
        weights.astype(jnp.bfloat16),
        heads_of_values,
        preferred_element_type=jnp.float32,
    )
    return (numerator / totals[..., None], maxima, totals)


def merge_all(local_output, local_maximum, local_sum, block_outs, block_maxima, block_sums):
    highest = jnp.maximum(local_maximum, jnp.max(block_maxima, axis=0))
    own_scale = local_sum * jnp.exp(local_maximum - highest)
    scales = block_sums * jnp.exp(block_maxima - highest[None])
    numerator = own_scale[..., None] * local_output + jnp.sum(
        scales[..., None] * block_outs.astype(jnp.float32), axis=0
    )
    return numerator / (own_scale + jnp.sum(scales, axis=0))[..., None]


def shards(
    residual,
    queries,
    keys,
    values,
    prefix_keys,
    cached_prefix_values,
    out_weight,
    norm_gain,
    w_gate,
    w_up,
    w_down,
    suffix_lengths,
    request_group,
    placement_order,
):
    tok_rows = queries.shape[0]
    key_value_width = keys.shape[1]
    span = prefix_keys.shape[1]
    block_keys = prefix_keys.shape[0] * span
    starts_at, ends_at, packed_group = row_layout(
        suffix_lengths[0], request_group[0], placement_order[0]
    )
    base_row = lax.axis_index("dev") * tok_rows
    own_rows = base_row + jnp.arange(tok_rows, dtype=jnp.int32)
    own_group, own_start = token_info(own_rows, starts_at, ends_at, packed_group)
    window = base_row - tok_rows + jnp.arange(2 * tok_rows, dtype=jnp.int32)
    suffix_mask = (window[None, :] >= own_start[:, None]) & (window[None, :] <= own_rows[:, None])
    key_group = jnp.arange(block_keys, dtype=jnp.int32) // span
    row_queries, row_keys, row_values = (
        lax.all_gather(queries, "dev", axis=0, tiled=True),
        lax.all_gather(keys, "dev", axis=0, tiled=True),
        lax.all_gather(values, "dev", axis=0, tiled=True),
    )
    prior_row = jnp.maximum(base_row - tok_rows, 0)
    before_keys = lax.dynamic_slice_in_dim(row_keys, prior_row, tok_rows, 0)
    before_values = lax.dynamic_slice_in_dim(row_values, prior_row, tok_rows, 0)
    local_output, local_maximum, local_sum = block_partial(
        queries,
        suffix_mask,
        jnp.concatenate([before_keys, keys], axis=0),
        jnp.concatenate([before_values, values], axis=0),
    )
    flat_keys = prefix_keys.reshape(block_keys, key_value_width)
    flat_values = cached_prefix_values.reshape(block_keys, key_value_width)
    row_count = row_queries.shape[0]
    row_group = token_info(
        jnp.arange(row_count, dtype=jnp.int32), starts_at, ends_at, packed_group
    )[0]
    step_rows = math.gcd(row_count, 512)

    def owner_block(block_index):
        first_row = block_index * step_rows
        rows_of_queries = lax.dynamic_slice_in_dim(row_queries, first_row, step_rows, 0)
        group_rows = lax.dynamic_slice_in_dim(row_group, first_row, step_rows, 0)
        allowed = group_rows[:, None] == key_group[None, :]
        part_out, maxima, totals = block_partial(rows_of_queries, allowed, flat_keys, flat_values)
        return (
            part_out.astype(jnp.bfloat16).reshape(step_rows, -1),
            maxima.reshape(step_rows, -1),
            totals.reshape(step_rows, -1),
        )

    part_outs, part_maxima, part_sums = lax.map(
        owner_block, jnp.arange(row_count // step_rows, dtype=jnp.int32)
    )
    peers = row_count // tok_rows
    part_outs = part_outs.reshape(peers, tok_rows, -1)
    part_maxima = part_maxima.reshape(peers, tok_rows, -1)
    part_sums = part_sums.reshape(peers, tok_rows, -1)
    back_outs = lax.all_to_all(part_outs, "dev", split_axis=0, concat_axis=0, tiled=True)
    back_maxima, back_sums = (
        lax.all_to_all(part_maxima, "dev", split_axis=0, concat_axis=0, tiled=True),
        lax.all_to_all(part_sums, "dev", split_axis=0, concat_axis=0, tiled=True),
    )
    merged = merge_all(
        local_output,
        local_maximum,
        local_sum,
        back_outs.reshape((peers,) + local_output.shape),
        back_maxima.reshape((peers,) + local_maximum.shape),
        back_sums.reshape((peers,) + local_sum.shape),
    )
    attention = merged.astype(jnp.bfloat16).reshape(tok_rows, -1)
    hidden_state = residual.astype(jnp.float32) + jnp.dot(
        attention, out_weight, preferred_element_type=jnp.float32
    )
    normed = (
        hidden_state
        * lax.rsqrt(jnp.mean(hidden_state * hidden_state, axis=-1, keepdims=True) + EPSILON)
        * norm_gain
    ).astype(jnp.bfloat16)
    full_gate, full_up, full_down = (
        lax.all_gather(w_gate, "grp", axis=0, tiled=True),
        lax.all_gather(w_up, "grp", axis=0, tiled=True),
        lax.all_gather(w_down, "grp", axis=1, tiled=True),
    )
    shard_piece = lax.all_gather(normed, "dev", axis=0, tiled=True)
    gate_value = jnp.dot(shard_piece, full_gate, preferred_element_type=jnp.float32)
    up_value = jnp.dot(shard_piece, full_up, preferred_element_type=jnp.float32)
    activation = (jax.nn.silu(gate_value) * up_value).astype(jnp.bfloat16)
    mlp_sum = lax.psum_scatter(
        jnp.dot(activation, full_down, preferred_element_type=jnp.float32).astype(jnp.bfloat16),
        "dev",
        scatter_dimension=0,
        tiled=True,
    ).astype(jnp.float32)
    return (hidden_state + mlp_sum).astype(jnp.bfloat16)


def solution(mesh):
    placed = (
        P(("grp", "dev"), None),
        P(("grp", "dev"), None),
        P(("grp", "dev"), None),
        P(("grp", "dev"), None),
        P("grp", "dev", None),
        P("grp", "dev", None),
        P(),
        P(),
        P("grp", "dev"),
        P("grp", "dev"),
        P("dev", "grp"),
        P("grp", None),
        P("grp", None),
        P("grp", None),
    )
    return jax.shard_map(
        shards, mesh=mesh, in_specs=placed, out_specs=P(("grp", "dev"), None), check_vma=False
    )
```

profile of v0, /device:TPU:0, one launch (start us, length us, event | category | flops | bytes accessed | tf_op | source)
XLA Modules:
  0.0 460.7 jit_solution(9504915503423663527)
XLA Ops:
  6.5 1.8 copy.63
  11.2 57.8 %all-gather.10.cloned.1.call-done = bf16[2048,1024]{0,1:T(8,128)(2,1)} async-done(((bf16[128,1024]{0,1:T(8,128)(2,1)}), bf16[2048,1024]{0,1:T(8,128)(2,1)}) %all-gather.10.cloned.1.call-update) | async-done | bytes 4194320 | tf_op jit(solution)/shard_map/all_gather | solution.py:96
  69.0 64.9 %while.15 = (s32[]{:T(128)}, bf16[4,512,1024]{2,1,0:T(8,128)(2,1)}, f32[4,512,16]{1,0,2:T(4,128)S(1)}, f32[4,512,16]{1,0,2:T(4,128)S(1)}, s32[4]{0:T(128)S(1)}, ...) while((s32[]{:T(128)}, bf16[4,512,1024]{2,1,0:T(8,128)(2,1)}, ...), condition=%wide.region_10.11_spmd.clone, body=%wide.region_7.10_spmd.clone.sunk | while | flops 561104896 | bytes 69378800 | solution.py:129
  70.3 1.3 constant_dynamic-slice_fusion.4
  71.6 1.1 reshape_reshape.10
  72.7 1.4 bitcast_reduce_fusion.2
  74.1 1.8 fusion.50
  75.9 1.4 copy-done
  77.5 5.6 %fusion.51 = bf16[512,4,4,64]{0,3,2,1:T(8,128)(2,1)S(1)} fusion(f32[4,512,4,256]{1,3,2,0:T(8,128)} %copy-done, f32[512,4,4]{0,2,1:T(4,128)S(1)} %get-tuple-element.183, pred[512,256]{0,1:T(8,128)(4,1)S(1)} %broadcast_compare_fusion.2, f32[512,4,4]{0,2,1:T(4,128)S(1)} %fusion.50, bf16[256,4,64,1]{2,1,0,3:T(4,128)(2,1)S(1)} %bitcast.111), kind=kOutput, calls=%fused_computation.10.clone.1 | convolution fusion | flops 277872640 | bytes 9764864 | tf_op jit(solution)/shard_map/while/body/eval_jaxpr/nkrm,mkd->nkrd/dot_general | solution.py:47
  83.7 1.1 constant_dynamic-update-slice_fusion.2
  86.6 1.3 constant_dynamic-slice_fusion.4
  87.9 1.1 reshape_reshape.10
  89.0 1.4 bitcast_reduce_fusion.2
  90.4 1.8 fusion.50
  92.2 1.4 copy-done
  93.8 5.6 %fusion.51 = bf16[512,4,4,64]{0,3,2,1:T(8,128)(2,1)S(1)} fusion(f32[4,512,4,256]{1,3,2,0:T(8,128)} %copy-done, f32[512,4,4]{0,2,1:T(4,128)S(1)} %get-tuple-element.183, pred[512,256]{0,1:T(8,128)(4,1)S(1)} %broadcast_compare_fusion.2, f32[512,4,4]{0,2,1:T(4,128)S(1)} %fusion.50, bf16[256,4,64,1]{2,1,0,3:T(4,128)(2,1)S(1)} %bitcast.111), kind=kOutput, calls=%fused_computation.10.clone.1 | convolution fusion | flops 277872640 | bytes 9764864 | tf_op jit(solution)/shard_map/while/body/eval_jaxpr/nkrm,mkd->nkrd/dot_general | solution.py:47
  99.9 1.0 constant_dynamic-update-slice_fusion.2
  102.8 1.3 constant_dynamic-slice_fusion.4
  104.1 1.1 reshape_reshape.10
  105.2 1.4 bitcast_reduce_fusion.2
  106.6 1.8 fusion.50
  108.4 1.4 copy-done
  110.0 5.6 %fusion.51 = bf16[512,4,4,64]{0,3,2,1:T(8,128)(2,1)S(1)} fusion(f32[4,512,4,256]{1,3,2,0:T(8,128)} %copy-done, f32[512,4,4]{0,2,1:T(4,128)S(1)} %get-tuple-element.183, pred[512,256]{0,1:T(8,128)(4,1)S(1)} %broadcast_compare_fusion.2, f32[512,4,4]{0,2,1:T(4,128)S(1)} %fusion.50, bf16[256,4,64,1]{2,1,0,3:T(4,128)(2,1)S(1)} %bitcast.111), kind=kOutput, calls=%fused_computation.10.clone.1 | convolution fusion | flops 277872640 | bytes 9764864 | tf_op jit(solution)/shard_map/while/body/eval_jaxpr/nkrm,mkd->nkrd/dot_general | solution.py:47
  116.1 1.1 constant_dynamic-update-slice_fusion.2
  119.1 1.3 constant_dynamic-slice_fusion.4
  120.4 1.1 reshape_reshape.10
  121.5 1.4 bitcast_reduce_fusion.2
  122.9 1.8 fusion.50
  124.6 1.4 copy-done
  126.2 5.6 %fusion.51 = bf16[512,4,4,64]{0,3,2,1:T(8,128)(2,1)S(1)} fusion(f32[4,512,4,256]{1,3,2,0:T(8,128)} %copy-done, f32[512,4,4]{0,2,1:T(4,128)S(1)} %get-tuple-element.183, pred[512,256]{0,1:T(8,128)(4,1)S(1)} %broadcast_compare_fusion.2, f32[512,4,4]{0,2,1:T(4,128)S(1)} %fusion.50, bf16[256,4,64,1]{2,1,0,3:T(4,128)(2,1)S(1)} %bitcast.111), kind=kOutput, calls=%fused_computation.10.clone.1 | convolution fusion | flops 277872640 | bytes 9764864 | tf_op jit(solution)/shard_map/while/body/eval_jaxpr/nkrm,mkd->nkrd/dot_general | solution.py:47
  132.3 1.1 constant_dynamic-update-slice_fusion.2
  134.6 4.9 %all-to-all-start = ((f32[16,128,16]{1,2,0:T(8,128)}), f32[16,128,16]{1,2,0:T(8,128)S(1)}, u32[]{:S(2)}, u32[]{:S(2)}) async-start(f32[16,128,16]{1,2,0:T(8,128)} %copy.66), calls=%async_computation | async-start | bytes 262144 | tf_op jit(solution)/shard_map/all_to_all | solution.py:138
  140.3 7.2 %all-to-all-done = f32[16,128,16]{1,2,0:T(8,128)S(1)} async-done(((f32[16,128,16]{1,2,0:T(8,128)}), f32[16,128,16]{1,2,0:T(8,128)S(1)}, u32[]{:S(2)}, u32[]{:S(2)}) %all-to-all-start) | async-done | bytes 131104 | tf_op jit(solution)/shard_map/all_to_all | solution.py:138
  147.6 3.5 all-to-all-start.1
  151.1 6.4 %copy.75 = bf16[16,128,1024]{1,2,0:T(8,128)(2,1)} copy(bf16[16,128,1024]{2,1,0:T(8,128)(2,1)} %bitcast.112) | data formatting | bytes 8388608 | tf_op jit(solution)/shard_map/reshape | solution.py:133
  157.5 1.9 all-to-all-done.1
  159.4 5.4 %all-to-all-start.2 = ((bf16[16,128,1024]{1,2,0:T(8,128)(2,1)}), bf16[16,128,1024]{1,2,0:T(8,128)(2,1)}, u32[]{:S(2)}, u32[]{:S(2)}) async-start(bf16[16,128,1024]{1,2,0:T(8,128)(2,1)} %copy.75), calls=%async_computation.2 | async-start | bytes 8388608 | tf_op jit(solution)/shard_map/all_to_all | solution.py:136
  165.9 1.0 constant_dynamic-slice_fusion.1
  168.3 50.7 %all-to-all-done.2 = bf16[16,128,1024]{1,2,0:T(8,128)(2,1)} async-done(((bf16[16,128,1024]{1,2,0:T(8,128)(2,1)}), bf16[16,128,1024]{1,2,0:T(8,128)(2,1)}, u32[]{:S(2)}, u32[]{:S(2)}) %all-to-all-start.2) | async-done | bytes 4194336 | tf_op jit(solution)/shard_map/all_to_all | solution.py:136
  219.0 3.2 fusion.16
  223.6 1.0 multiply_convert_fusion.1
  226.0 68.2 %all-gather.14.cloned.1.call-done = bf16[2048,2048]{1,0:T(8,128)(2,1)} async-done(((bf16[128,2048]{1,0:T(8,128)(2,1)}), bf16[2048,2048]{1,0:T(8,128)(2,1)}) %all-gather.14.cloned.1.call-update) | async-done | bytes 8388624 | tf_op jit(solution)/shard_map/all_gather | solution.py:163
  294.2 10.4 %fusion.30 = f32[2048,512]{1,0:T(8,128)} fusion(bf16[2048,2048]{1,0:T(8,128)(2,1)} %all-gather.14.cloned.1.call-done, bf16[2048,512]{1,0:T(8,128)(2,1)} %all-gather.16.cloned.1.call-done), kind=kOutput, calls=%fused_computation.64 | convolution fusion | flops 4294967296 | bytes 14680064 | tf_op jit(solution)/shard_map/dot_general | solution.py:164
  304.6 16.0 %all-gather.18.cloned.1.call-done = bf16[2048,512]{1,0:T(8,128)(2,1)} async-done(((bf16[256,512]{1,0:T(8,128)(2,1)}), bf16[2048,512]{1,0:T(8,128)(2,1)}) %all-gather.18.cloned.1.call-update) | async-done | bytes 2097168 | tf_op jit(solution)/shard_map/all_gather | solution.py:160
  320.6 28.9 %all-gather.20.cloned.1.call-done = bf16[512,2048]{1,0:T(8,128)(2,1)} async-done(((bf16[512,256]{1,0:T(8,128)(2,1)}), bf16[512,2048]{1,0:T(8,128)(2,1)}) %all-gather.20.cloned.1.call-update) | async-done | bytes 2097168 | tf_op jit(solution)/shard_map/all_gather | solution.py:161
  349.5 15.2 %convolution_convert_fusion = bf16[2048,2048]{1,0:T(8,128)(2,1)} fusion(bf16[512,2048]{1,0:T(8,128)(2,1)} %all-gather.20.cloned.1.call-done, f32[2048,512]{1,0:T(8,128)} %fusion.30, bf16[2048,2048]{1,0:T(8,128)(2,1)} %all-gather.14.cloned.1.call-done, bf16[2048,512]{1,0:T(8,128)(2,1)} %all-gather.18.cloned.1.call-done), kind=kOutput, calls=%fused_computation.25 | convolution fusion | flops 8600420352 | bytes 25165824 | tf_op jit(solution)/shard_map/dot_general | solution.py:168
  364.8 87.2 %reduce-scatter.2.cloned.1.call-done = bf16[128,2048]{1,0:T(8,128)(2,1)} async-done(((bf16[2048,2048]{1,0:T(8,128)(2,1)}), bf16[128,2048]{1,0:T(8,128)(2,1)}) %reduce-scatter.2.cloned.1.call-update) | async-done | bytes 524304 | tf_op jit(solution)/shard_map/reduce_scatter | solution.py:167
  451.9 1.9 add_convert_fusion
  (118 shorter events, 17.1 us)
Async XLA Ops:
  6.5 62.4 %all-gather.10.cloned.1.call-start = ((), (), s32[]{:S(2)}) async-start(), calls=%async_computation.5 | async-start | bytes 4456448 | tf_op jit(solution)/shard_map/all_gather | solution.py:96
  8.4 157.6 %all-gather.12.cloned.1.call-start = ((), (), s32[]{:S(2)}) async-start(), calls=%async_computation.6 | async-start | bytes 1114112 | tf_op jit(solution)/shard_map/all_gather | solution.py:98
  9.1 156.8 %all-gather.8.cloned.1.call-start = ((), (), s32[]{:S(2)}) async-start(), calls=%async_computation.4 | async-start | bytes 1114112 | tf_op jit(solution)/shard_map/all_gather | solution.py:97
  74.1 3.2 copy-start
  74.1 3.2 copy-start.2
  90.4 3.2 copy-start
  90.4 3.2 copy-start.2
  106.6 3.2 copy-start
  106.6 3.2 copy-start.2
  122.8 3.2 copy-start
  122.9 3.2 copy-start.2
  134.6 12.9 %all-to-all-start = ((f32[16,128,16]{1,2,0:T(8,128)}), f32[16,128,16]{1,2,0:T(8,128)S(1)}, u32[]{:S(2)}, u32[]{:S(2)}) async-start(f32[16,128,16]{1,2,0:T(8,128)} %copy.66), calls=%async_computation | async-start | bytes 262144 | tf_op jit(solution)/shard_map/all_to_all | solution.py:138
  147.6 11.8 %all-to-all-start.1 = ((f32[16,128,16]{1,2,0:T(8,128)}), f32[16,128,16]{1,2,0:T(8,128)S(1)}, u32[]{:S(2)}, u32[]{:S(2)}) async-start(f32[16,128,16]{1,2,0:T(8,128)} %copy.70), calls=%async_computation.1 | async-start | bytes 262144 | tf_op jit(solution)/shard_map/all_to_all | solution.py:139
  157.5 9.4 %copy-start.5 = (bf16[128,256]{1,0:T(8,128)(2,1)S(1)}, bf16[128,256]{1,0:T(8,128)(2,1)}, u32[]{:S(2)}) copy-start(bf16[128,256]{1,0:T(8,128)(2,1)} %param.18) | copy-start | bytes 196612
  157.5 9.5 %copy-start.6 = (bf16[128,256]{1,0:T(8,128)(2,1)S(1)}, bf16[128,256]{1,0:T(8,128)(2,1)}, u32[]{:S(2)}) copy-start(bf16[128,256]{1,0:T(8,128)(2,1)} %param.19) | copy-start | bytes 196612
  157.5 9.7 %copy-start.3 = (bf16[128,1024]{0,1:T(8,128)(2,1)S(1)}, bf16[128,1024]{0,1:T(8,128)(2,1)}, u32[]{:S(2)}) copy-start(bf16[128,1024]{0,1:T(8,128)(2,1)} %copy.63) | copy-start | bytes 786436
  159.4 59.6 %all-to-all-start.2 = ((bf16[16,128,1024]{1,2,0:T(8,128)(2,1)}), bf16[16,128,1024]{1,2,0:T(8,128)(2,1)}, u32[]{:S(2)}, u32[]{:S(2)}) async-start(bf16[16,128,1024]{1,2,0:T(8,128)(2,1)} %copy.75), calls=%async_computation.2 | async-start | bytes 8388608 | tf_op jit(solution)/shard_map/all_to_all | solution.py:136
  164.9 61.1 %all-gather.16.cloned.1.call-start = ((), (), s32[]{:S(2)}) async-start(), calls=%async_computation.8 | async-start | bytes 2359296 | tf_op jit(solution)/shard_map/all_gather | solution.py:159
  165.4 128.8 %all-gather.14.cloned.1.call-start = ((), (), s32[]{:S(2)}) async-start(), calls=%async_computation.7 | async-start | bytes 8912896 | tf_op jit(solution)/shard_map/all_gather | solution.py:163
  168.3 54.4 %copy-start.4 = (bf16[128,2048]{1,0:T(8,128)(2,1)S(1)}, bf16[128,2048]{1,0:T(8,128)(2,1)}, u32[]{:S(2)}) copy-start(bf16[128,2048]{1,0:T(8,128)(2,1)} %param.16) | copy-start | bytes 1572868
  219.0 3.7 copy-start.1
  222.7 0.9 copy-start.7
  224.6 96.1 %all-gather.18.cloned.1.call-start = ((), (), s32[]{:S(2)}) async-start(), calls=%async_computation.9 | async-start | bytes 2359296 | tf_op jit(solution)/shard_map/all_gather | solution.py:160
  225.2 124.3 %all-gather.20.cloned.1.call-start = ((), (), s32[]{:S(2)}) async-start(), calls=%async_computation.10 | async-start | bytes 2359296 | tf_op jit(solution)/shard_map/all_gather | solution.py:161
  225.9 226.0 %reduce-scatter.2.cloned.1.call-start = ((), (), s32[]{:S(2)}) async-start(), calls=%async_computation.11 | async-start | bytes 8912896 | tf_op jit(solution)/shard_map/reduce_scatter | solution.py:167
Sparse Core Ops, SparseCore 0:
  9.4 59.4 all-gather.9
  71.1 41.8 all-gather.11
  115.2 42.2 all-gather.7
  167.1 26.6 all-gather.15
  224.7 69.4 all-gather.13
  295.8 24.8 all-gather.17
  322.3 27.1 all-gather.19
  364.9 87.0 reduce-scatter.1
where the time goes:
time: 462 us; the launch traced here: 461 us
  waiting for transfers between devices  321 us (69%)
  matrix products  55.4 us (12%)
  local copies, waits for them, and re-layouts  37.8 us (8%)
  other arithmetic  15.6 us (3%)
  starting transfers between devices  14.3 us (3%)
  between operations  13.8 us (3%)
    reduce_scatter x1, waiting for transfers between devices, shards(): lax.psum_scatter(jnp.dot(activation, full_down, preferred_element_type=jn...  87.2 us
    all_gather x1, waiting for transfers between devices, shards(): shard_piece = lax.all_gather(normed, 'dev', axis=0, tiled=True)  68.2 us
    all_gather x1, waiting for transfers between devices, shards(): lax.all_gather(queries, 'dev', axis=0, tiled=True)  57.8 us
    all_to_all x1, waiting for transfers between devices, shards(): lax.all_to_all(part_outs, 'dev', split_axis=0, concat_axis=0, tiled=True)  50.7 us
    all_gather x1, waiting for transfers between devices, shards(): lax.all_gather(w_down, 'grp', axis=1, tiled=True)  28.9 us
    dot_general x5, matrix products, block_partial(): jnp.einsum('nkrm,mkd->nkrd', weights.astype(jnp.bfloat16), heads_of_value...  22.8 us
    all_gather x1, waiting for transfers between devices, shards(): lax.all_gather(w_up, 'grp', axis=0, tiled=True)  16 us
    dot_general x1, matrix products, shards(): jnp.dot(activation, full_down, preferred_element_type=jnp.float32)  15.2 us
  transfers between devices with their start and end apart: 11, of which 8 were waited for; matrix products, arithmetic and copies ran while one was open for 18% of the time, Pallas kernels for 0%

commit v1 on v0

--- a/solution.py
+++ b/solution.py
@@ -7,6 +7,11 @@
 HEAD_SIZE = 64
 NEG_FILL = -1e30
 EPSILON = 1e-05
+
+
+def all_by_exchange(array, axis, along):
+    stack = jnp.stack([array] * lax.axis_size(axis))
+    return jnp.concatenate(lax.all_to_all(stack, axis, 0, 0), axis=along)
 
 
 def row_layout(lengths, group_map, packed_order):
@@ -157,7 +162,7 @@
     ).astype(jnp.bfloat16)
     full_gate, full_up, full_down = (
         lax.all_gather(w_gate, "grp", axis=0, tiled=True),
-        lax.all_gather(w_up, "grp", axis=0, tiled=True),
+        all_by_exchange(w_up, "grp", 0),
         lax.all_gather(w_down, "grp", axis=1, tiled=True),
     )
     shard_piece = lax.all_gather(normed, "dev", axis=0, tiled=True)

time: 462 us -> 434 us (0.939)
  waiting for transfers between devices: 321 us -> 288 us
    all_gather x1 -> x0, waiting for transfers between devices: 16 us -> none  [shards(): lax.all_gather(w_up, 'grp', axis=0, tiled=True)]
    all_gather x1, waiting for transfers between devices: 28.9 us -> 17.4 us  [shards(): lax.all_gather(w_down, 'grp', axis=1, tiled=True)]
    all_gather x1, waiting for transfers between devices: 68.2 us -> 63.2 us  [shards(): shard_piece = lax.all_gather(normed, 'dev', axis=0, tiled=True)]
  transfers between devices with their start and end apart: 11 -> 11, of which waited for: 8 -> 7; matrix products, arithmetic and copies ran while one was open for 18% -> 20% of each run, Pallas kernels for 0% -> 0%
where the time goes in v1:
time: 434 us; the launch traced here: 433 us
  waiting for transfers between devices  288 us (66%)
  matrix products  54.8 us (13%)
  local copies, waits for them, and re-layouts  39.3 us (9%)
  starting transfers between devices  18.6 us (4%)
  other arithmetic  15.6 us (4%)
  between operations  13.8 us (3%)
    reduce_scatter x1, waiting for transfers between devices, shards(): lax.psum_scatter(jnp.dot(activation, full_down, preferred_element_type=jn...  87 us
    all_gather x1, waiting for transfers between devices, shards(): shard_piece = lax.all_gather(normed, 'dev', axis=0, tiled=True)  63.2 us
    all_gather x1, waiting for transfers between devices, shards(): lax.all_gather(queries, 'dev', axis=0, tiled=True)  57.8 us
    all_to_all x1, waiting for transfers between devices, shards(): lax.all_to_all(part_outs, 'dev', split_axis=0, concat_axis=0, tiled=True)  50.7 us
    dot_general x5, matrix products, block_partial(): jnp.einsum('nkrm,mkd->nkrd', weights.astype(jnp.bfloat16), heads_of_value...  22.8 us
    all_gather x1, waiting for transfers between devices, shards(): lax.all_gather(w_down, 'grp', axis=1, tiled=True)  17.4 us
    dot_general x1, matrix products, shards(): jnp.dot(activation, full_down, preferred_element_type=jnp.float32)  14.7 us
    dot_general x1, matrix products, shards(): jnp.dot(shard_piece, full_gate, preferred_element_type=jnp.float32)  10.4 us
  transfers between devices with their start and end apart: 11, of which 7 were waited for; matrix products, arithmetic and copies ran while one was open for 20% of the time, Pallas kernels for 0%

profile of v1, /device:TPU:0, one launch (start us, length us, event | category | flops | bytes accessed | tf_op | source)
XLA Modules:
  0.0 432.5 jit_solution(21062000987882008)
XLA Ops:
  6.5 1.8 copy.63
  11.2 57.8 %all-gather.9.cloned.1.call-done = bf16[2048,1024]{0,1:T(8,128)(2,1)} async-done(((bf16[128,1024]{0,1:T(8,128)(2,1)}), bf16[2048,1024]{0,1:T(8,128)(2,1)}) %all-gather.9.cloned.1.call-update) | async-done | bytes 4194320 | tf_op jit(solution)/shard_map/all_gather | solution.py:101
  69.0 64.9 %while.15 = (s32[]{:T(128)}, bf16[4,512,1024]{2,1,0:T(8,128)(2,1)}, f32[4,512,16]{1,0,2:T(4,128)S(1)}, f32[4,512,16]{1,0,2:T(4,128)S(1)}, s32[4]{0:T(128)S(1)}, ...) while((s32[]{:T(128)}, bf16[4,512,1024]{2,1,0:T(8,128)(2,1)}, ...), condition=%wide.region_10.11_spmd.clone, body=%wide.region_7.10_spmd.clone.sunk | while | flops 561104896 | bytes 69378800 | solution.py:134
  70.3 1.3 constant_dynamic-slice_fusion.4
  71.6 1.1 reshape_reshape.10
  72.7 1.4 bitcast_reduce_fusion.2
  74.1 1.8 fusion.50
  75.9 1.4 copy-done
  77.5 5.6 %fusion.51 = bf16[512,4,4,64]{0,3,2,1:T(8,128)(2,1)S(1)} fusion(f32[4,512,4,256]{1,3,2,0:T(8,128)} %copy-done, f32[512,4,4]{0,2,1:T(4,128)S(1)} %get-tuple-element.183, pred[512,256]{0,1:T(8,128)(4,1)S(1)} %broadcast_compare_fusion.2, f32[512,4,4]{0,2,1:T(4,128)S(1)} %fusion.50, bf16[256,4,64,1]{2,1,0,3:T(4,128)(2,1)S(1)} %bitcast.112), kind=kOutput, calls=%fused_computation.10.clone.1 | convolution fusion | flops 277872640 | bytes 9764864 | tf_op jit(solution)/shard_map/while/body/eval_jaxpr/nkrm,mkd->nkrd/dot_general | solution.py:52
  83.7 1.1 constant_dynamic-update-slice_fusion.2
  86.6 1.3 constant_dynamic-slice_fusion.4
  87.9 1.1 reshape_reshape.10
  89.0 1.4 bitcast_reduce_fusion.2
  90.4 1.8 fusion.50
  92.2 1.4 copy-done
  93.8 5.6 %fusion.51 = bf16[512,4,4,64]{0,3,2,1:T(8,128)(2,1)S(1)} fusion(f32[4,512,4,256]{1,3,2,0:T(8,128)} %copy-done, f32[512,4,4]{0,2,1:T(4,128)S(1)} %get-tuple-element.183, pred[512,256]{0,1:T(8,128)(4,1)S(1)} %broadcast_compare_fusion.2, f32[512,4,4]{0,2,1:T(4,128)S(1)} %fusion.50, bf16[256,4,64,1]{2,1,0,3:T(4,128)(2,1)S(1)} %bitcast.112), kind=kOutput, calls=%fused_computation.10.clone.1 | convolution fusion | flops 277872640 | bytes 9764864 | tf_op jit(solution)/shard_map/while/body/eval_jaxpr/nkrm,mkd->nkrd/dot_general | solution.py:52
  99.9 1.0 constant_dynamic-update-slice_fusion.2
  102.8 1.3 constant_dynamic-slice_fusion.4
  104.1 1.1 reshape_reshape.10
  105.2 1.4 bitcast_reduce_fusion.2
  106.6 1.8 fusion.50
  108.4 1.4 copy-done
  110.0 5.6 %fusion.51 = bf16[512,4,4,64]{0,3,2,1:T(8,128)(2,1)S(1)} fusion(f32[4,512,4,256]{1,3,2,0:T(8,128)} %copy-done, f32[512,4,4]{0,2,1:T(4,128)S(1)} %get-tuple-element.183, pred[512,256]{0,1:T(8,128)(4,1)S(1)} %broadcast_compare_fusion.2, f32[512,4,4]{0,2,1:T(4,128)S(1)} %fusion.50, bf16[256,4,64,1]{2,1,0,3:T(4,128)(2,1)S(1)} %bitcast.112), kind=kOutput, calls=%fused_computation.10.clone.1 | convolution fusion | flops 277872640 | bytes 9764864 | tf_op jit(solution)/shard_map/while/body/eval_jaxpr/nkrm,mkd->nkrd/dot_general | solution.py:52
  116.1 1.1 constant_dynamic-update-slice_fusion.2
  119.1 1.3 constant_dynamic-slice_fusion.4
  120.4 1.1 reshape_reshape.10
  121.5 1.4 bitcast_reduce_fusion.2
  122.9 1.8 fusion.50
  124.6 1.4 copy-done
  126.2 5.6 %fusion.51 = bf16[512,4,4,64]{0,3,2,1:T(8,128)(2,1)S(1)} fusion(f32[4,512,4,256]{1,3,2,0:T(8,128)} %copy-done, f32[512,4,4]{0,2,1:T(4,128)S(1)} %get-tuple-element.183, pred[512,256]{0,1:T(8,128)(4,1)S(1)} %broadcast_compare_fusion.2, f32[512,4,4]{0,2,1:T(4,128)S(1)} %fusion.50, bf16[256,4,64,1]{2,1,0,3:T(4,128)(2,1)S(1)} %bitcast.112), kind=kOutput, calls=%fused_computation.10.clone.1 | convolution fusion | flops 277872640 | bytes 9764864 | tf_op jit(solution)/shard_map/while/body/eval_jaxpr/nkrm,mkd->nkrd/dot_general | solution.py:52
  132.3 1.1 constant_dynamic-update-slice_fusion.2
  134.6 4.9 %all-to-all-start = ((f32[16,128,16]{1,2,0:T(8,128)}), f32[16,128,16]{1,2,0:T(8,128)S(1)}, u32[]{:S(2)}, u32[]{:S(2)}) async-start(f32[16,128,16]{1,2,0:T(8,128)} %copy.66), calls=%async_computation | async-start | bytes 262144 | tf_op jit(solution)/shard_map/all_to_all | solution.py:143
  140.3 7.2 %all-to-all-done = f32[16,128,16]{1,2,0:T(8,128)S(1)} async-done(((f32[16,128,16]{1,2,0:T(8,128)}), f32[16,128,16]{1,2,0:T(8,128)S(1)}, u32[]{:S(2)}, u32[]{:S(2)}) %all-to-all-start) | async-done | bytes 131104 | tf_op jit(solution)/shard_map/all_to_all | solution.py:143
  147.6 3.5 all-to-all-start.1
  151.1 6.4 %copy.75 = bf16[16,128,1024]{1,2,0:T(8,128)(2,1)} copy(bf16[16,128,1024]{2,1,0:T(8,128)(2,1)} %bitcast.113) | data formatting | bytes 8388608 | tf_op jit(solution)/shard_map/reshape | solution.py:138
  157.5 1.9 all-to-all-done.1
  159.4 5.4 %all-to-all-start.2 = ((bf16[16,128,1024]{1,2,0:T(8,128)(2,1)}), bf16[16,128,1024]{1,2,0:T(8,128)(2,1)}, u32[]{:S(2)}, u32[]{:S(2)}) async-start(bf16[16,128,1024]{1,2,0:T(8,128)(2,1)} %copy.75), calls=%async_computation.2 | async-start | bytes 8388608 | tf_op jit(solution)/shard_map/all_to_all | solution.py:141
  165.9 1.0 constant_dynamic-slice_fusion.1
  168.3 50.7 %all-to-all-done.2 = bf16[16,128,1024]{1,2,0:T(8,128)(2,1)} async-done(((bf16[16,128,1024]{1,2,0:T(8,128)(2,1)}), bf16[16,128,1024]{1,2,0:T(8,128)(2,1)}, u32[]{:S(2)}, u32[]{:S(2)}) %all-to-all-start.2) | async-done | bytes 4194336 | tf_op jit(solution)/shard_map/all_to_all | solution.py:141
  219.0 3.2 fusion.16
  225.2 1.5 stack.2
  226.7 4.3 all-to-all-start.3
  231.0 63.2 %all-gather.13.cloned.1.call-done = bf16[2048,2048]{1,0:T(8,128)(2,1)} async-done(((bf16[128,2048]{1,0:T(8,128)(2,1)}), bf16[2048,2048]{1,0:T(8,128)(2,1)}) %all-gather.13.cloned.1.call-update) | async-done | bytes 8388624 | tf_op jit(solution)/shard_map/all_gather | solution.py:168
  294.2 10.4 %fusion.30 = f32[2048,512]{1,0:T(8,128)} fusion(bf16[2048,2048]{1,0:T(8,128)(2,1)} %all-gather.13.cloned.1.call-done, bf16[2048,512]{1,0:T(8,128)(2,1)} %all-gather.15.cloned.1.call-done), kind=kOutput, calls=%fused_computation.64 | convolution fusion | flops 4294967296 | bytes 14680064 | tf_op jit(solution)/shard_map/dot_general | solution.py:169
  304.7 17.4 %all-gather.17.cloned.1.call-done = bf16[512,2048]{1,0:T(8,128)(2,1)} async-done(((bf16[512,256]{1,0:T(8,128)(2,1)}), bf16[512,2048]{1,0:T(8,128)(2,1)}) %all-gather.17.cloned.1.call-update) | async-done | bytes 2097168 | tf_op jit(solution)/shard_map/all_gather | solution.py:166
  322.1 14.7 %convolution_convert_fusion = bf16[2048,2048]{1,0:T(8,128)(2,1)} fusion(bf16[512,2048]{1,0:T(8,128)(2,1)} %all-gather.17.cloned.1.call-done, f32[2048,512]{1,0:T(8,128)} %fusion.30, bf16[2048,2048]{1,0:T(8,128)(2,1)} %all-gather.13.cloned.1.call-done, bf16[2048,512]{1,0:T(8,128)(2,1)S(1)} %bitcast.115), kind=kOutput, calls=%fused_computation.25 | convolution fusion | flops 8600420352 | bytes 25165824 | tf_op jit(solution)/shard_map/dot_general | solution.py:173
  336.8 87.0 %reduce-scatter.2.cloned.1.call-done = bf16[128,2048]{1,0:T(8,128)(2,1)} async-done(((bf16[2048,2048]{1,0:T(8,128)(2,1)}), bf16[128,2048]{1,0:T(8,128)(2,1)}) %reduce-scatter.2.cloned.1.call-update) | async-done | bytes 524304 | tf_op jit(solution)/shard_map/reduce_scatter | solution.py:172
  423.7 1.9 add_convert_fusion
  (120 shorter events, 17.3 us)
Async XLA Ops:
  6.5 62.4 %all-gather.9.cloned.1.call-start = ((), (), s32[]{:S(2)}) async-start(), calls=%async_computation.6 | async-start | bytes 4456448 | tf_op jit(solution)/shard_map/all_gather | solution.py:101
  8.4 157.6 %all-gather.11.cloned.1.call-start = ((), (), s32[]{:S(2)}) async-start(), calls=%async_computation.7 | async-start | bytes 1114112 | tf_op jit(solution)/shard_map/all_gather | solution.py:103
  9.1 156.8 %all-gather.7.cloned.1.call-start = ((), (), s32[]{:S(2)}) async-start(), calls=%async_computation.5 | async-start | bytes 1114112 | tf_op jit(solution)/shard_map/all_gather | solution.py:102
  74.1 3.2 copy-start
  74.1 3.2 copy-start.2
  90.4 3.2 copy-start
  90.4 3.2 copy-start.2
  106.6 3.2 copy-start
  106.6 3.2 copy-start.2
  122.8 3.2 copy-start
  122.9 3.2 copy-start.2
  134.6 12.9 %all-to-all-start = ((f32[16,128,16]{1,2,0:T(8,128)}), f32[16,128,16]{1,2,0:T(8,128)S(1)}, u32[]{:S(2)}, u32[]{:S(2)}) async-start(f32[16,128,16]{1,2,0:T(8,128)} %copy.66), calls=%async_computation | async-start | bytes 262144 | tf_op jit(solution)/shard_map/all_to_all | solution.py:143
  147.6 11.8 %all-to-all-start.1 = ((f32[16,128,16]{1,2,0:T(8,128)}), f32[16,128,16]{1,2,0:T(8,128)S(1)}, u32[]{:S(2)}, u32[]{:S(2)}) async-start(f32[16,128,16]{1,2,0:T(8,128)} %copy.70), calls=%async_computation.1 | async-start | bytes 262144 | tf_op jit(solution)/shard_map/all_to_all | solution.py:144
  157.5 9.4 %copy-start.6 = (bf16[128,256]{1,0:T(8,128)(2,1)S(1)}, bf16[128,256]{1,0:T(8,128)(2,1)}, u32[]{:S(2)}) copy-start(bf16[128,256]{1,0:T(8,128)(2,1)} %param.18) | copy-start | bytes 196612
  157.5 9.5 %copy-start.7 = (bf16[128,256]{1,0:T(8,128)(2,1)S(1)}, bf16[128,256]{1,0:T(8,128)(2,1)}, u32[]{:S(2)}) copy-start(bf16[128,256]{1,0:T(8,128)(2,1)} %param.19) | copy-start | bytes 196612
  157.5 9.7 %copy-start.3 = (bf16[128,1024]{0,1:T(8,128)(2,1)S(1)}, bf16[128,1024]{0,1:T(8,128)(2,1)}, u32[]{:S(2)}) copy-start(bf16[128,1024]{0,1:T(8,128)(2,1)} %copy.63) | copy-start | bytes 786436
  159.4 59.6 %all-to-all-start.2 = ((bf16[16,128,1024]{1,2,0:T(8,128)(2,1)}), bf16[16,128,1024]{1,2,0:T(8,128)(2,1)}, u32[]{:S(2)}, u32[]{:S(2)}) async-start(bf16[16,128,1024]{1,2,0:T(8,128)(2,1)} %copy.75), calls=%async_computation.2 | async-start | bytes 8388608 | tf_op jit(solution)/shard_map/all_to_all | solution.py:141
  164.9 66.2 %all-gather.15.cloned.1.call-start = ((), (), s32[]{:S(2)}) async-start(), calls=%async_computation.9 | async-start | bytes 2359296 | tf_op jit(solution)/shard_map/all_gather | solution.py:164
  165.4 128.8 %all-gather.13.cloned.1.call-start = ((), (), s32[]{:S(2)}) async-start(), calls=%async_computation.8 | async-start | bytes 8912896 | tf_op jit(solution)/shard_map/all_gather | solution.py:168
  168.3 54.4 %copy-start.4 = (bf16[128,2048]{1,0:T(8,128)(2,1)S(1)}, bf16[128,2048]{1,0:T(8,128)(2,1)}, u32[]{:S(2)}) copy-start(bf16[128,2048]{1,0:T(8,128)(2,1)} %param.16) | copy-start | bytes 1572868
  219.0 3.7 copy-start.1
  222.7 0.9 copy-start.8
  222.8 2.4 copy-start.5
  224.6 97.5 %all-gather.17.cloned.1.call-start = ((), (), s32[]{:S(2)}) async-start(), calls=%async_computation.10 | async-start | bytes 2359296 | tf_op jit(solution)/shard_map/all_gather | solution.py:166
  226.7 78.0 %all-to-all-start.3 = ((bf16[8,256,512]{2,1,0:T(8,128)(2,1)}), bf16[8,256,512]{2,1,0:T(8,128)(2,1)S(1)}, u32[]{:S(2)}, u32[]{:S(2)}) async-start(bf16[8,256,512]{2,1,0:T(8,128)(2,1)} %stack.2), calls=%async_computation.3 | async-start | bytes 4194304 | tf_op jit(solution)/shard_map/all_to_all | solution.py:14
  231.0 192.8 %reduce-scatter.2.cloned.1.call-start = ((), (), s32[]{:S(2)}) async-start(), calls=%async_computation.11 | async-start | bytes 8912896 | tf_op jit(solution)/shard_map/reduce_scatter | solution.py:172
Sparse Core Ops, SparseCore 0:
  9.4 59.4 all-gather.8
  71.1 41.8 all-gather.10
  115.2 42.2 all-gather.6
  167.1 26.6 all-gather.14
  224.7 69.4 all-gather.12
  295.7 26.3 all-gather.16
  336.9 86.7 reduce-scatter.1
